TPU v7x, 128 devices: a whole 4x4x4 slice. The times are simulated.
128 devices in a mesh: wide: 16 (over x, z), narrow: 8 (over y, core).
Axes of the slice: x: 4, y: 4, z: 4, core: 2. Of those that a mesh axis runs over, the one named last changes fastest.
Arguments:
- tensor_slab: float32 [512, 512, 2048], P(None, 'wide', 'narrow'), may hold values from -220 to 220
- start_basis: float32 [512, 64], replicated, may hold values from -6 to 6
Outputs:
- factor_basis: float32 [512, 64], replicated
- core_unfold: float32 [2048, 64, 512], P('narrow', 'wide')
All inputs are finite; a program needn't handle non-finite values.
Results may differ from a plain program's by a relative error of at most 0.0003.
Values sent between devices are 32-bit elements; how exact they have to be, the bound alone decides.
A program may use at most 64 MiB of HBM per device.

v0:
```python
import jax
import jax.numpy as jnp
from jax import lax
from jax.sharding import PartitionSpec as P

I1 = 512
ITERS = 8


def orthonormal(block, inner):
    lower_factor = jnp.linalg.cholesky(inner)
    return jax.scipy.linalg.solve_triangular(lower_factor, block.T, lower=True).T


def shards(tensor_slab, start_basis):
    highest = lax.Precision.HIGHEST
    unfold = tensor_slab.reshape(I1, -1)
    basis = start_basis
    local_gram = jnp.dot(unfold, unfold.T, precision=highest, preferred_element_type=jnp.float32)
    gram_full = lax.psum(local_gram, ("wide", "narrow"))
    for sweep_index in range(ITERS):
        block = jnp.dot(gram_full, basis, precision=highest)
        basis = orthonormal(block, jnp.dot(block.T, block, precision=highest))
    core_local = jnp.einsum("ir,ijl->lrj", basis, tensor_slab, precision=highest)
    core_unfold = lax.all_to_all(core_local, "wide", split_axis=1, concat_axis=2, tiled=True)
    return (basis, core_unfold)


def solution(mesh):
    placed = (P(None, "wide", "narrow"), P())
    return jax.shard_map(
        shards,
        mesh=mesh,
        in_specs=placed,
        out_specs=(P(), P("narrow", "wide", None)),
        check_vma=False,
    )
```

profile of v0, /device:TPU:1, one launch (start us, length us, event | category | flops | bytes accessed | tf_op | source)
XLA Modules:
  0.0 389.1 jit_solution(11629814040123961032)
XLA Ops:
  7.2 40.1 %fusion.7 = f32[512,512]{1,0:T(8,128)} fusion(f32[512,32,256]{2,1,0:T(8,128)} %param.5), kind=kOutput, calls=%fused_computation.5 | convolution fusion | flops 25769803776 | bytes 17825792 | tf_op jit(solution)/shard_map/dot_general | solution.py:19
  47.3 150.7 %all-reduce.2.cloned.1.call-done = f32[512,512]{1,0:T(8,128)} async-done(((f32[512,512]{1,0:T(8,128)}), f32[512,512]{1,0:T(8,128)}) %all-reduce.2.cloned.1.call-update) | async-done | bytes 1048592 | tf_op jit(solution)/shard_map/psum | solution.py:20
  200.7 5.8 %cholesky.134 = f32[64,64]{1,0:T(8,128)S(1)} custom-call(f32[64,64]{1,0:T(8,128)S(1)} %fusion.50), custom_call_target="Cholesky" | custom-call | tf_op jit(solution)/shard_map/jit(cholesky)/cholesky | solution.py:11
  207.9 4.9 %custom-call.12 = f32[1,64,64]{1,2,0:T(8,128)S(1)} custom-call(f32[1,64,64]{2,1,0:T(8,128)S(1)} %fusion.27), custom_call_target="InvertDiagBlocksLowerTriangular" | custom-call | tf_op jit(solution)/shard_map/jit(_solve_triangular)/triangular_solve | solution.py:12
  213.2 2.4 fusion.67
  215.9 5.8 %cholesky.145 = f32[64,64]{1,0:T(8,128)S(1)} custom-call(f32[64,64]{1,0:T(8,128)S(1)} %fusion.48), custom_call_target="Cholesky" | custom-call | tf_op jit(solution)/shard_map/jit(cholesky)/cholesky | solution.py:11
  223.1 4.9 %custom-call.13 = f32[1,64,64]{1,2,0:T(8,128)S(1)} custom-call(f32[1,64,64]{2,1,0:T(8,128)S(1)} %fusion.28), custom_call_target="InvertDiagBlocksLowerTriangular" | custom-call | tf_op jit(solution)/shard_map/jit(_solve_triangular)/triangular_solve | solution.py:12
  231.0 5.8 %cholesky.156 = f32[64,64]{1,0:T(8,128)S(1)} custom-call(f32[64,64]{1,0:T(8,128)S(1)} %fusion.46), custom_call_target="Cholesky" | custom-call | tf_op jit(solution)/shard_map/jit(cholesky)/cholesky | solution.py:11
  238.2 4.9 %custom-call.14 = f32[1,64,64]{1,2,0:T(8,128)S(1)} custom-call(f32[1,64,64]{2,1,0:T(8,128)S(1)} %fusion.29), custom_call_target="InvertDiagBlocksLowerTriangular" | custom-call | tf_op jit(solution)/shard_map/jit(_solve_triangular)/triangular_solve | solution.py:12
  243.5 2.4 fusion.71
  246.2 5.8 %cholesky.167 = f32[64,64]{1,0:T(8,128)S(1)} custom-call(f32[64,64]{1,0:T(8,128)S(1)} %fusion.44), custom_call_target="Cholesky" | custom-call | tf_op jit(solution)/shard_map/jit(cholesky)/cholesky | solution.py:11
  253.4 4.9 %custom-call.15 = f32[1,64,64]{1,2,0:T(8,128)S(1)} custom-call(f32[1,64,64]{2,1,0:T(8,128)S(1)} %fusion.30), custom_call_target="InvertDiagBlocksLowerTriangular" | custom-call | tf_op jit(solution)/shard_map/jit(_solve_triangular)/triangular_solve | solution.py:12
  258.6 2.5 fusion.73
  261.5 5.8 %cholesky.178 = f32[64,64]{1,0:T(8,128)S(1)} custom-call(f32[64,64]{1,0:T(8,128)S(1)} %fusion.42), custom_call_target="Cholesky" | custom-call | tf_op jit(solution)/shard_map/jit(cholesky)/cholesky | solution.py:11
  268.7 4.9 %custom-call.16 = f32[1,64,64]{1,2,0:T(8,128)S(1)} custom-call(f32[1,64,64]{2,1,0:T(8,128)S(1)} %fusion.31), custom_call_target="InvertDiagBlocksLowerTriangular" | custom-call | tf_op jit(solution)/shard_map/jit(_solve_triangular)/triangular_solve | solution.py:12
  273.9 2.4 fusion.75
  276.6 5.8 %cholesky.189 = f32[64,64]{1,0:T(8,128)S(1)} custom-call(f32[64,64]{1,0:T(8,128)S(1)} %fusion.40), custom_call_target="Cholesky" | custom-call | tf_op jit(solution)/shard_map/jit(cholesky)/cholesky | solution.py:11
  283.8 4.9 %custom-call.17 = f32[1,64,64]{1,2,0:T(8,128)S(1)} custom-call(f32[1,64,64]{2,1,0:T(8,128)S(1)} %fusion.32), custom_call_target="InvertDiagBlocksLowerTriangular" | custom-call | tf_op jit(solution)/shard_map/jit(_solve_triangular)/triangular_solve | solution.py:12
  291.8 5.8 %cholesky.200 = f32[64,64]{1,0:T(8,128)S(1)} custom-call(f32[64,64]{1,0:T(8,128)S(1)} %fusion.38), custom_call_target="Cholesky" | custom-call | tf_op jit(solution)/shard_map/jit(cholesky)/cholesky | solution.py:11
  299.0 4.9 %custom-call.18 = f32[1,64,64]{1,2,0:T(8,128)S(1)} custom-call(f32[1,64,64]{2,1,0:T(8,128)S(1)} %fusion.33), custom_call_target="InvertDiagBlocksLowerTriangular" | custom-call | tf_op jit(solution)/shard_map/jit(_solve_triangular)/triangular_solve | solution.py:12
  306.9 5.8 %cholesky.211 = f32[64,64]{1,0:T(8,128)S(1)} custom-call(f32[64,64]{1,0:T(8,128)S(1)} %fusion.36), custom_call_target="Cholesky" | custom-call | tf_op jit(solution)/shard_map/jit(cholesky)/cholesky | solution.py:11
  314.1 4.9 %custom-call.19 = f32[1,64,64]{1,2,0:T(8,128)S(1)} custom-call(f32[1,64,64]{2,1,0:T(8,128)S(1)} %fusion.34), custom_call_target="InvertDiagBlocksLowerTriangular" | custom-call | tf_op jit(solution)/shard_map/jit(_solve_triangular)/triangular_solve | solution.py:12
  319.4 25.8 %fusion.4 = f32[256,64,32]{0,1,2:T(8,128)S(1)} fusion(f32[512,32,256]{2,1,0:T(8,128)} %param.5, f32[64,512]{1,0:T(8,128)S(1)} %fusion.11), kind=kOutput, calls=%fused_computation.4 | convolution fusion | flops 3221225472 | bytes 19005440 | tf_op jit(solution)/shard_map/ir,ijl->lrj/dot_general | solution.py:24
  346.4 33.5 %all_to_all.18 = f32[256,64,32]{0,2,1:T(8,128)S(1)} all-to-all(f32[256,64,32]{0,2,1:T(8,128)S(1)} %copy.53), channel_id=1, replica_groups=mesh['wide'=16,'narrow'=8] {'wide'}, dimensions={1} | all-to-all | bytes 4194304 | tf_op jit(solution)/shard_map/all_to_all | solution.py:25
  (69 shorter events, 28.9 us)
Async XLA Ops:
  7.2 190.9 %copy-start = (f32[512,64]{0,1:T(8,128)S(1)}, f32[512,64]{0,1:T(8,128)}, u32[]{:S(2)}) copy-start(f32[512,64]{0,1:T(8,128)} %param.6) | copy-start | bytes 393220
  7.2 190.9 %all-reduce.2.cloned.1.call-start = ((), (), s32[]{:S(2)}) async-start(), calls=%async_computation.1 | async-start | bytes 2097152 | tf_op jit(solution)/shard_map/psum | solution.py:20
  319.4 62.7 %copy-start.1 = (f32[64,512]{1,0:T(8,128)}, f32[64,512]{1,0:T(8,128)S(1)}, u32[]{:S(2)}) copy-start(f32[64,512]{1,0:T(8,128)S(1)} %fusion.11) | copy-start | bytes 393220
Sparse Core Ops, SparseCore 0:
  47.4 150.5 all-reduce.1
where the time goes:
time: 393 us; the launch traced here: 389 us
  waiting for transfers between devices  151 us (38%)
  other arithmetic  96.6 us (25%)
  matrix products  89.7 us (23%)
  blocking collectives  33.5 us (9%)
  between operations  14.6 us (4%)
  local copies, waits for them, and re-layouts  3.93 us (1%)
    psum x1, waiting for transfers between devices, shards(): gram_full = lax.psum(local_gram, ('wide', 'narrow'))  151 us
    another operation x24, other arithmetic, orthonormal(): lower_factor = jnp.linalg.cholesky(inner)  52.2 us
    another operation x16, other arithmetic, orthonormal(): jax.scipy.linalg.solve_triangular(lower_factor, block.T, lower=True)  44.4 us
    dot_general x1, matrix products, shards(): jnp.dot(unfold, unfold.T, precision=highest, preferred_element_type=jnp.f...  40.1 us
    all_to_all x1, blocking collectives, shards(): lax.all_to_all(core_local, 'wide', split_axis=1, concat_axis=2, tiled=True)  33.5 us
    dot_general x1, matrix products, shards(): jnp.einsum('ir,ijl->lrj', basis, tensor_slab, precision=highest)  25.8 us
    dot_general x8, matrix products, shards(): block = jnp.dot(gram_full, basis, precision=highest)  19 us
  transfers between devices with their start and end apart: 1, of which 1 were waited for; matrix products, arithmetic and copies ran while one was open for 0% of the time, Pallas kernels for 0%

commit v1 on v0

--- a/solution.py
+++ b/solution.py
@@ -22,7 +22,12 @@
         block = jnp.dot(gram_full, basis, precision=highest)
         basis = orthonormal(block, jnp.dot(block.T, block, precision=highest))
     core_local = jnp.einsum("ir,ijl->lrj", basis, tensor_slab, precision=highest)
-    core_unfold = lax.all_to_all(core_local, "wide", split_axis=1, concat_axis=2, tiled=True)
+    core_unfold = jnp.concatenate(
+        lax.all_to_all(
+            jnp.stack(jnp.split(core_local, lax.axis_size("wide"), axis=1)), "wide", 0, 0
+        ),
+        axis=2,
+    )
     return (basis, core_unfold)
 
 

time: 393 us -> 384 us (0.977)
  matrix products: 89.7 us -> 81.3 us
    dot_general x8, matrix products: 19 us -> 10.6 us  [shards(): block = jnp.dot(gram_full, basis, precision=highest)]
where the time goes in v1:
time: 384 us; the launch traced here: 381 us
  waiting for transfers between devices  151 us (39%)
  other arithmetic  96.6 us (25%)
  matrix products  81.3 us (21%)
  blocking collectives  33.5 us (9%)
  between operations  14.7 us (4%)
    psum x1, waiting for transfers between devices, shards(): gram_full = lax.psum(local_gram, ('wide', 'narrow'))  151 us
    another operation x24, other arithmetic, orthonormal(): lower_factor = jnp.linalg.cholesky(inner)  52.2 us
    another operation x16, other arithmetic, orthonormal(): jax.scipy.linalg.solve_triangular(lower_factor, block.T, lower=True)  44.4 us
    dot_general x1, matrix products, shards(): jnp.dot(unfold, unfold.T, precision=highest, preferred_element_type=jnp.f...  40.1 us
    all_to_all x1, blocking collectives, shards(): lax.all_to_all(jnp.stack(jnp.split(core_local, lax.axis_size('wide'), axi...  33.5 us
    dot_general x1, matrix products, shards(): jnp.einsum('ir,ijl->lrj', basis, tensor_slab, precision=highest)  25.8 us
    dot_general x8, matrix products, shards(): block = jnp.dot(gram_full, basis, precision=highest)  10.6 us
  transfers between devices with their start and end apart: 1, of which 1 were waited for; matrix products, arithmetic and copies ran while one was open for 0% of the time, Pallas kernels for 0%

profile of v1, /device:TPU:1, one launch (start us, length us, event | category | flops | bytes accessed | tf_op | source)
XLA Modules:
  0.0 380.5 jit_solution(2024902462358372228)
XLA Ops:
  7.2 40.1 %fusion.7 = f32[512,512]{1,0:T(8,128)} fusion(f32[512,32,256]{2,1,0:T(8,128)} %param.5), kind=kOutput, calls=%fused_computation.5 | convolution fusion | flops 25769803776 | bytes 17825792 | tf_op jit(solution)/shard_map/dot_general | solution.py:19
  47.3 150.7 %all-reduce.2.cloned.1.call-done = f32[512,512]{1,0:T(8,128)} async-done(((f32[512,512]{1,0:T(8,128)}), f32[512,512]{1,0:T(8,128)}) %all-reduce.2.cloned.1.call-update) | async-done | bytes 1048592 | tf_op jit(solution)/shard_map/psum | solution.py:20
  198.0 2.4 fusion.81
  200.8 5.8 %cholesky.134 = f32[64,64]{1,0:T(8,128)S(1)} custom-call(f32[64,64]{1,0:T(8,128)S(1)} %fusion.66), custom_call_target="Cholesky" | custom-call | tf_op jit(solution)/shard_map/jit(cholesky)/cholesky | solution.py:11
  208.0 4.9 %custom-call.12 = f32[1,64,64]{1,2,0:T(8,128)S(1)} custom-call(f32[1,64,64]{2,1,0:T(8,128)S(1)} %fusion.43), custom_call_target="InvertDiagBlocksLowerTriangular" | custom-call | tf_op jit(solution)/shard_map/jit(_solve_triangular)/triangular_solve | solution.py:12
  214.8 5.8 %cholesky.145 = f32[64,64]{1,0:T(8,128)S(1)} custom-call(f32[64,64]{1,0:T(8,128)S(1)} %fusion.64), custom_call_target="Cholesky" | custom-call | tf_op jit(solution)/shard_map/jit(cholesky)/cholesky | solution.py:11
  222.0 4.9 %custom-call.13 = f32[1,64,64]{1,2,0:T(8,128)S(1)} custom-call(f32[1,64,64]{2,1,0:T(8,128)S(1)} %fusion.44), custom_call_target="InvertDiagBlocksLowerTriangular" | custom-call | tf_op jit(solution)/shard_map/jit(_solve_triangular)/triangular_solve | solution.py:12
  227.2 1.1 fusion.85
  228.7 5.8 %cholesky.156 = f32[64,64]{1,0:T(8,128)S(1)} custom-call(f32[64,64]{1,0:T(8,128)S(1)} %fusion.62), custom_call_target="Cholesky" | custom-call | tf_op jit(solution)/shard_map/jit(cholesky)/cholesky | solution.py:11
  235.9 4.9 %custom-call.14 = f32[1,64,64]{1,2,0:T(8,128)S(1)} custom-call(f32[1,64,64]{2,1,0:T(8,128)S(1)} %fusion.45), custom_call_target="InvertDiagBlocksLowerTriangular" | custom-call | tf_op jit(solution)/shard_map/jit(_solve_triangular)/triangular_solve | solution.py:12
  242.6 5.8 %cholesky.167 = f32[64,64]{1,0:T(8,128)S(1)} custom-call(f32[64,64]{1,0:T(8,128)S(1)} %fusion.60), custom_call_target="Cholesky" | custom-call | tf_op jit(solution)/shard_map/jit(cholesky)/cholesky | solution.py:11
  249.8 4.9 %custom-call.15 = f32[1,64,64]{1,2,0:T(8,128)S(1)} custom-call(f32[1,64,64]{2,1,0:T(8,128)S(1)} %fusion.46), custom_call_target="InvertDiagBlocksLowerTriangular" | custom-call | tf_op jit(solution)/shard_map/jit(_solve_triangular)/triangular_solve | solution.py:12
  255.1 1.3 fusion.89
  256.7 5.8 %cholesky.178 = f32[64,64]{1,0:T(8,128)S(1)} custom-call(f32[64,64]{1,0:T(8,128)S(1)} %fusion.58), custom_call_target="Cholesky" | custom-call | tf_op jit(solution)/shard_map/jit(cholesky)/cholesky | solution.py:11
  263.9 4.9 %custom-call.16 = f32[1,64,64]{1,2,0:T(8,128)S(1)} custom-call(f32[1,64,64]{2,1,0:T(8,128)S(1)} %fusion.47), custom_call_target="InvertDiagBlocksLowerTriangular" | custom-call | tf_op jit(solution)/shard_map/jit(_solve_triangular)/triangular_solve | solution.py:12
  270.7 5.8 %cholesky.189 = f32[64,64]{1,0:T(8,128)S(1)} custom-call(f32[64,64]{1,0:T(8,128)S(1)} %fusion.56), custom_call_target="Cholesky" | custom-call | tf_op jit(solution)/shard_map/jit(cholesky)/cholesky | solution.py:11
  277.8 4.9 %custom-call.17 = f32[1,64,64]{1,2,0:T(8,128)S(1)} custom-call(f32[1,64,64]{2,1,0:T(8,128)S(1)} %fusion.48), custom_call_target="InvertDiagBlocksLowerTriangular" | custom-call | tf_op jit(solution)/shard_map/jit(_solve_triangular)/triangular_solve | solution.py:12
  284.6 5.8 %cholesky.200 = f32[64,64]{1,0:T(8,128)S(1)} custom-call(f32[64,64]{1,0:T(8,128)S(1)} %fusion.54), custom_call_target="Cholesky" | custom-call | tf_op jit(solution)/shard_map/jit(cholesky)/cholesky | solution.py:11
  291.8 4.9 %custom-call.18 = f32[1,64,64]{1,2,0:T(8,128)S(1)} custom-call(f32[1,64,64]{2,1,0:T(8,128)S(1)} %fusion.49), custom_call_target="InvertDiagBlocksLowerTriangular" | custom-call | tf_op jit(solution)/shard_map/jit(_solve_triangular)/triangular_solve | solution.py:12
  298.5 5.8 %cholesky.211 = f32[64,64]{1,0:T(8,128)S(1)} custom-call(f32[64,64]{1,0:T(8,128)S(1)} %fusion.52), custom_call_target="Cholesky" | custom-call | tf_op jit(solution)/shard_map/jit(cholesky)/cholesky | solution.py:11
  305.7 4.9 %custom-call.19 = f32[1,64,64]{1,2,0:T(8,128)S(1)} custom-call(f32[1,64,64]{2,1,0:T(8,128)S(1)} %fusion.50), custom_call_target="InvertDiagBlocksLowerTriangular" | custom-call | tf_op jit(solution)/shard_map/jit(_solve_triangular)/triangular_solve | solution.py:12
  311.0 25.8 %fusion.4 = f32[256,64,32]{0,1,2:T(8,128)S(1)} fusion(f32[512,32,256]{2,1,0:T(8,128)} %param.5, f32[64,512]{1,0:T(8,128)S(1)} %fusion.27), kind=kOutput, calls=%fused_computation.4 | convolution fusion | flops 3221225472 | bytes 19005440 | tf_op jit(solution)/shard_map/ir,ijl->lrj/dot_general | solution.py:24
  337.5 33.5 %all_to_all.5 = f32[16,256,4,32]{1,2,3,0:T(4,128)S(1)} all-to-all(f32[16,256,4,32]{1,2,3,0:T(4,128)S(1)} %fusion.10), channel_id=1, replica_groups=mesh['wide'=16,'narrow'=8] {'wide'}, dimensions={0} | all-to-all | bytes 4194304 | tf_op jit(solution)/shard_map/all_to_all | solution.py:26
  371.0 2.5 copy.15
  (85 shorter events, 22.4 us)
Async XLA Ops:
  7.2 190.9 %copy-start = (f32[512,64]{0,1:T(8,128)S(1)}, f32[512,64]{0,1:T(8,128)}, u32[]{:S(2)}) copy-start(f32[512,64]{0,1:T(8,128)} %param.6) | copy-start | bytes 393220
  7.2 190.9 %all-reduce.2.cloned.1.call-start = ((), (), s32[]{:S(2)}) async-start(), calls=%async_computation.1 | async-start | bytes 2097152 | tf_op jit(solution)/shard_map/psum | solution.py:20
  198.0 15.2 %copy-start.1 = (f32[512,512]{1,0:T(8,128)S(1)}, f32[512,512]{1,0:T(8,128)}, u32[]{:S(2)}) copy-start(f32[512,512]{1,0:T(8,128)} %all-reduce.2.cloned.1.call-done) | copy-start | bytes 3145732
  310.9 25.8 %copy-start.2 = (f32[64,512]{1,0:T(8,128)}, f32[64,512]{1,0:T(8,128)S(1)}, u32[]{:S(2)}) copy-start(f32[64,512]{1,0:T(8,128)S(1)} %fusion.27) | copy-start | bytes 393220
Sparse Core Ops, SparseCore 0:
  47.4 150.5 all-reduce.1

commit v2 on v0

--- a/solution.py
+++ b/solution.py
@@ -17,7 +17,7 @@
     unfold = tensor_slab.reshape(I1, -1)
     basis = start_basis
     local_gram = jnp.dot(unfold, unfold.T, precision=highest, preferred_element_type=jnp.float32)
-    gram_full = lax.psum(local_gram, ("wide", "narrow"))
+    gram_full = lax.psum(lax.psum(local_gram, "narrow"), "wide")
     for sweep_index in range(ITERS):
         block = jnp.dot(gram_full, basis, precision=highest)
         basis = orthonormal(block, jnp.dot(block.T, block, precision=highest))

time: 393 us -> 395 us (level)
    psum x1 -> x2, waiting for transfers between devices: 151 us -> 154 us  [shards(): gram_full = lax.psum(lax.psum(local_gram, 'narrow'), 'wide')]
  transfers between devices with their start and end apart: 1 -> 2, of which waited for: 1 -> 2; matrix products, arithmetic and copies ran while one was open for 0% -> 0% of each run, Pallas kernels for 0% -> 0%
where the time goes in v2:
time: 395 us; the launch traced here: 388 us
  waiting for transfers between devices  154 us (39%)
  other arithmetic  96.6 us (24%)
  matrix products  89.3 us (23%)
  blocking collectives  29.7 us (8%)
  between operations  14.6 us (4%)
    psum x2, waiting for transfers between devices, shards(): gram_full = lax.psum(lax.psum(local_gram, 'narrow'), 'wide')  154 us
    another operation x24, other arithmetic, orthonormal(): lower_factor = jnp.linalg.cholesky(inner)  52.2 us
    another operation x16, other arithmetic, orthonormal(): jax.scipy.linalg.solve_triangular(lower_factor, block.T, lower=True)  44.4 us
    dot_general x1, matrix products, shards(): jnp.dot(unfold, unfold.T, precision=highest, preferred_element_type=jnp.f...  39.6 us
    all_to_all x1, blocking collectives, shards(): lax.all_to_all(core_local, 'wide', split_axis=1, concat_axis=2, tiled=True)  29.7 us
    dot_general x1, matrix products, shards(): jnp.einsum('ir,ijl->lrj', basis, tensor_slab, precision=highest)  25.8 us
    dot_general x8, matrix products, shards(): block = jnp.dot(gram_full, basis, precision=highest)  19 us
  transfers between devices with their start and end apart: 2, of which 2 were waited for; matrix products, arithmetic and copies ran while one was open for 0% of the time, Pallas kernels for 0%

profile of v2, /device:TPU:1, one launch (start us, length us, event | category | flops | bytes accessed | tf_op | source)
XLA Modules:
  0.0 388.3 jit_solution(10088945790546932113)
XLA Ops:
  7.2 39.6 %fusion.7 = f32[512,512]{1,0:T(8,128)} fusion(f32[512,32,256]{2,1,0:T(8,128)} %param.5), kind=kOutput, calls=%fused_computation.5 | convolution fusion | flops 25769803776 | bytes 17825792 | tf_op jit(solution)/shard_map/dot_general | solution.py:19
  47.4 63.3 %all-reduce.3.cloned.1.call-done = f32[512,512]{1,0:T(8,128)} async-done(((f32[512,512]{1,0:T(8,128)}), f32[512,512]{1,0:T(8,128)}) %all-reduce.3.cloned.1.call-update) | async-done | bytes 1048592 | tf_op jit(solution)/shard_map/psum | solution.py:20
  110.7 90.3 %all-reduce.5.cloned.1.call-done = f32[512,512]{1,0:T(8,128)} async-done(((f32[512,512]{1,0:T(8,128)}), f32[512,512]{1,0:T(8,128)}) %all-reduce.5.cloned.1.call-update) | async-done | bytes 1048592 | tf_op jit(solution)/shard_map/psum | solution.py:20
  203.7 5.8 %cholesky.134 = f32[64,64]{1,0:T(8,128)S(1)} custom-call(f32[64,64]{1,0:T(8,128)S(1)} %fusion.50), custom_call_target="Cholesky" | custom-call | tf_op jit(solution)/shard_map/jit(cholesky)/cholesky | solution.py:11
  210.9 4.9 %custom-call.12 = f32[1,64,64]{1,2,0:T(8,128)S(1)} custom-call(f32[1,64,64]{2,1,0:T(8,128)S(1)} %fusion.27), custom_call_target="InvertDiagBlocksLowerTriangular" | custom-call | tf_op jit(solution)/shard_map/jit(_solve_triangular)/triangular_solve | solution.py:12
  216.1 2.4 fusion.67
  218.8 5.8 %cholesky.145 = f32[64,64]{1,0:T(8,128)S(1)} custom-call(f32[64,64]{1,0:T(8,128)S(1)} %fusion.48), custom_call_target="Cholesky" | custom-call | tf_op jit(solution)/shard_map/jit(cholesky)/cholesky | solution.py:11
  226.0 4.9 %custom-call.13 = f32[1,64,64]{1,2,0:T(8,128)S(1)} custom-call(f32[1,64,64]{2,1,0:T(8,128)S(1)} %fusion.28), custom_call_target="InvertDiagBlocksLowerTriangular" | custom-call | tf_op jit(solution)/shard_map/jit(_solve_triangular)/triangular_solve | solution.py:12
  231.3 2.4 fusion.69
  234.0 5.8 %cholesky.156 = f32[64,64]{1,0:T(8,128)S(1)} custom-call(f32[64,64]{1,0:T(8,128)S(1)} %fusion.46), custom_call_target="Cholesky" | custom-call | tf_op jit(solution)/shard_map/jit(cholesky)/cholesky | solution.py:11
  241.2 4.9 %custom-call.14 = f32[1,64,64]{1,2,0:T(8,128)S(1)} custom-call(f32[1,64,64]{2,1,0:T(8,128)S(1)} %fusion.29), custom_call_target="InvertDiagBlocksLowerTriangular" | custom-call | tf_op jit(solution)/shard_map/jit(_solve_triangular)/triangular_solve | solution.py:12
  249.1 5.8 %cholesky.167 = f32[64,64]{1,0:T(8,128)S(1)} custom-call(f32[64,64]{1,0:T(8,128)S(1)} %fusion.44), custom_call_target="Cholesky" | custom-call | tf_op jit(solution)/shard_map/jit(cholesky)/cholesky | solution.py:11
  256.3 4.9 %custom-call.15 = f32[1,64,64]{1,2,0:T(8,128)S(1)} custom-call(f32[1,64,64]{2,1,0:T(8,128)S(1)} %fusion.30), custom_call_target="InvertDiagBlocksLowerTriangular" | custom-call | tf_op jit(solution)/shard_map/jit(_solve_triangular)/triangular_solve | solution.py:12
  261.6 2.5 fusion.73
  264.5 5.8 %cholesky.178 = f32[64,64]{1,0:T(8,128)S(1)} custom-call(f32[64,64]{1,0:T(8,128)S(1)} %fusion.42), custom_call_target="Cholesky" | custom-call | tf_op jit(solution)/shard_map/jit(cholesky)/cholesky | solution.py:11
  271.6 4.9 %custom-call.16 = f32[1,64,64]{1,2,0:T(8,128)S(1)} custom-call(f32[1,64,64]{2,1,0:T(8,128)S(1)} %fusion.31), custom_call_target="InvertDiagBlocksLowerTriangular" | custom-call | tf_op jit(solution)/shard_map/jit(_solve_triangular)/triangular_solve | solution.py:12
  279.6 5.8 %cholesky.189 = f32[64,64]{1,0:T(8,128)S(1)} custom-call(f32[64,64]{1,0:T(8,128)S(1)} %fusion.40), custom_call_target="Cholesky" | custom-call | tf_op jit(solution)/shard_map/jit(cholesky)/cholesky | solution.py:11
  286.8 4.9 %custom-call.17 = f32[1,64,64]{1,2,0:T(8,128)S(1)} custom-call(f32[1,64,64]{2,1,0:T(8,128)S(1)} %fusion.32), custom_call_target="InvertDiagBlocksLowerTriangular" | custom-call | tf_op jit(solution)/shard_map/jit(_solve_triangular)/triangular_solve | solution.py:12
  294.7 5.8 %cholesky.200 = f32[64,64]{1,0:T(8,128)S(1)} custom-call(f32[64,64]{1,0:T(8,128)S(1)} %fusion.38), custom_call_target="Cholesky" | custom-call | tf_op jit(solution)/shard_map/jit(cholesky)/cholesky | solution.py:11
  301.9 4.9 %custom-call.18 = f32[1,64,64]{1,2,0:T(8,128)S(1)} custom-call(f32[1,64,64]{2,1,0:T(8,128)S(1)} %fusion.33), custom_call_target="InvertDiagBlocksLowerTriangular" | custom-call | tf_op jit(solution)/shard_map/jit(_solve_triangular)/triangular_solve | solution.py:12
  309.9 5.8 %cholesky.211 = f32[64,64]{1,0:T(8,128)S(1)} custom-call(f32[64,64]{1,0:T(8,128)S(1)} %fusion.36), custom_call_target="Cholesky" | custom-call | tf_op jit(solution)/shard_map/jit(cholesky)/cholesky | solution.py:11
  317.1 4.9 %custom-call.19 = f32[1,64,64]{1,2,0:T(8,128)S(1)} custom-call(f32[1,64,64]{2,1,0:T(8,128)S(1)} %fusion.34), custom_call_target="InvertDiagBlocksLowerTriangular" | custom-call | tf_op jit(solution)/shard_map/jit(_solve_triangular)/triangular_solve | solution.py:12
  322.3 25.8 %fusion.4 = f32[256,64,32]{0,1,2:T(8,128)S(1)} fusion(f32[512,32,256]{2,1,0:T(8,128)} %param.5, f32[64,512]{1,0:T(8,128)S(1)} %fusion.11), kind=kOutput, calls=%fused_computation.4 | convolution fusion | flops 3221225472 | bytes 19005440 | tf_op jit(solution)/shard_map/ir,ijl->lrj/dot_general | solution.py:24
  349.4 29.7 %all_to_all.18 = f32[256,64,32]{0,2,1:T(8,128)S(1)} all-to-all(f32[256,64,32]{0,2,1:T(8,128)S(1)} %copy.53), channel_id=1, replica_groups=mesh['wide'=16,'narrow'=8] {'wide'}, dimensions={1} | all-to-all | bytes 4194304 | tf_op jit(solution)/shard_map/all_to_all | solution.py:25
  (72 shorter events, 31.8 us)
Async XLA Ops:
  7.2 193.8 %copy-start = (f32[512,64]{0,1:T(8,128)S(1)}, f32[512,64]{0,1:T(8,128)}, u32[]{:S(2)}) copy-start(f32[512,64]{0,1:T(8,128)} %param.6) | copy-start | bytes 393220
  7.2 103.5 %all-reduce.3.cloned.1.call-start = ((), (), s32[]{:S(2)}) async-start(), calls=%async_computation.1 | async-start | bytes 2097152 | tf_op jit(solution)/shard_map/psum | solution.py:20
  46.9 154.1 %all-reduce.5.cloned.1.call-start = ((), (), s32[]{:S(2)}) async-start(), calls=%async_computation.2 | async-start | bytes 2097152 | tf_op jit(solution)/shard_map/psum | solution.py:20
  322.3 58.9 %copy-start.1 = (f32[64,512]{1,0:T(8,128)}, f32[64,512]{1,0:T(8,128)S(1)}, u32[]{:S(2)}) copy-start(f32[64,512]{1,0:T(8,128)S(1)} %fusion.11) | copy-start | bytes 393220
Sparse Core Ops, SparseCore 0:
  47.0 63.6 all-reduce.2
  113.9 86.9 all-reduce.4
